TPU v7x, 256 devices: a whole 4x4x8 slice. The times are simulated.
256 devices in a mesh: cfg: 2 (over x_lo), seq: 128 (over y, z, x_hi, core).
Axes of the slice: x: 4 (x_hi: 2, x_lo: 2; x = x_hi * 2 + x_lo), y: 4, z: 8, core: 2. Of those that a mesh axis runs over, the one named last changes fastest.
Arguments:
- queries: bfloat16 [2, 4608, 1536], P('cfg', 'seq'), may hold values from -25 to 25
- keys: bfloat16 [2, 4608, 1536], P('cfg', 'seq'), may hold values from -25 to 25
- values: bfloat16 [2, 4608, 1536], P('cfg', 'seq'), may hold values from -6 to 6
- residual: bfloat16 [2, 4608, 3072], P('cfg', 'seq'), may hold values from -4 to 4
- gate: float32 [2, 3072], P('cfg'), may hold values from 0.5 to 4
- text_len: int32 [2], P('cfg'), may hold values from 64 to 512
- w_out: bfloat16 [1536, 3072], replicated, may hold values from -0.15625 to 0.15625
- w_final: bfloat16 [3072, 64], replicated, may hold values from -0.109375 to 0.109375
- latent: float32 [128, 2048], P('seq', 'cfg'), may hold values from -6 to 6
- owner: int32 [128], replicated, may hold values from 0 to 127, as said below
Outputs:
- hidden_out: bfloat16 [2, 4608, 3072], P('cfg', 'seq')
- latent_next: float32 [128, 2048], P('seq', 'cfg')
Inputs may be any that keep to these rules, and one draw needn't show every extreme that they name: `owner`: a permutation of the indices of seq.
All inputs are finite; a program needn't handle non-finite values.
Results may differ from a plain program's by a relative error of at most 0.0065.
Values may be sent and summed in bfloat16 or wider, within the bound.
A program may use at most 192 MiB of HBM per device.

v0:
```python
import jax
import jax.numpy as jnp
from jax import lax
from jax.sharding import PartitionSpec as P

HEADS = 12
HEAD = 128
CH = 64


def partner_2(x, axis, distance):
    return lax.ppermute(x, axis, [(i, i ^ 1 << distance) for i in range(lax.axis_size(axis))])


def local(queries, keys, values, residual, gate, text_len, w_out, w_final, latent, owner):
    qloc = queries[0]
    kloc = keys[0]
    vloc = values[0]
    tokens, width = qloc.shape
    nseq = lax.axis_size("seq")
    myself = lax.axis_index("seq")
    seqlen = tokens * nseq
    textslots = seqlen // 9
    limit = text_len[0]
    scale = HEAD ** (-0.5)
    both = lax.all_gather(jnp.concatenate([kloc, vloc], axis=1), "seq", axis=0, tiled=True)
    qheads = qloc.reshape(tokens, HEADS, HEAD)
    kall = both[:, :width].reshape(seqlen, HEADS, HEAD)
    vall = both[:, width:].reshape(seqlen, HEADS, HEAD)
    keypos = jnp.arange(seqlen, dtype=jnp.int32)
    valid = (keypos >= textslots) | (keypos < limit)
    scores = jnp.einsum("qhd,khd->hqk", qheads, kall, preferred_element_type=jnp.float32) * scale
    scores = jnp.where(valid[None, None, :], scores, -1e30)
    top = jnp.max(scores, axis=2, keepdims=True)
    expo = jnp.where(valid[None, None, :], jnp.exp(scores - top), 0.0)
    total = jnp.sum(expo, axis=2, keepdims=True)
    accum = jnp.einsum(
        "hqk,khd->hqd", expo.astype(jnp.bfloat16), vall, preferred_element_type=jnp.float32
    )
    attn = (accum / total).astype(jnp.bfloat16).transpose(1, 0, 2).reshape(tokens, width)
    proj = jnp.dot(attn, w_out, preferred_element_type=jnp.float32)
    stream = (residual[0].astype(jnp.float32) + gate[0][None, :] * proj).astype(jnp.bfloat16)
    is_cond = lax.axis_index("cfg") == 0
    speed = jnp.dot(stream, w_final, preferred_element_type=jnp.float32)
    other = partner_2(speed, "cfg", 0)
    speed_cond = jnp.where(is_cond, speed, other)
    speed_free = jnp.where(is_cond, other, speed)
    guided = speed_free + 3.0 * (speed_cond - speed_free)
    gathered = lax.all_gather(guided, "seq", axis=0, tiled=True)
    columns = latent.shape[1]
    tilerows = columns * lax.axis_size("cfg") // CH
    mytile = jnp.sum(jnp.where(owner == myself, jnp.arange(nseq, dtype=jnp.int32), 0))
    picked = lax.dynamic_slice_in_dim(gathered, textslots + mytile * tilerows, tilerows, 0)
    flat = picked.reshape(tilerows * CH)
    mine = lax.dynamic_slice_in_dim(flat, lax.axis_index("cfg") * columns, columns, 0)
    latent_next = latent - 0.25 * mine.reshape(1, columns)
    return (stream[None], latent_next)


def solution(mesh):
    placed = (
        P("cfg", "seq", None),
        P("cfg", "seq", None),
        P("cfg", "seq", None),
        P("cfg", "seq", None),
        P("cfg", None),
        P("cfg"),
        P(),
        P(),
        P("seq", "cfg"),
        P(),
    )
    return jax.shard_map(
        local,
        mesh=mesh,
        in_specs=placed,
        out_specs=(P("cfg", "seq", None), P("seq", "cfg")),
        check_vma=False,
    )
```

profile of v0, /device:TPU:1, one launch (start us, length us, event | category | flops | bytes accessed | tf_op | source)
XLA Modules:
  0.0 468.3 jit_solution(7332716834692380684)
XLA Ops:
  7.2 0.0 copy-start
  7.2 0.0 all-gather.5.cloned.1.call-start
  7.2 1.7 maximum_bitcast_fusion
  8.9 0.0 all-gather.5.cloned.1.call-update
  9.0 0.0 all-gather.7.cloned.1.call-start
  9.7 1.0 reshape_squeeze.3
  10.7 210.0 %all-gather.5.cloned.1.call-done = bf16[128,36,3072]{2,1,0:T(8,128)(2,1)} async-done(((bf16[1,36,3072]{2,1,0:T(8,128)(2,1)}), bf16[128,36,3072]{2,1,0:T(8,128)(2,1)}) %all-gather.5.cloned.1.call-update) | async-done | bytes 28311568 | tf_op jit(solution)/shard_map/all_gather | solution.py:26
  220.7 33.4 %reshape.35 = bf16[4608,3072]{1,0:T(8,128)(2,1)} reshape(bf16[128,36,3072]{2,1,0:T(8,128)(2,1)} %all-gather.5.cloned.1.call-done) | data formatting | bytes 56623104
  254.1 20.7 %fusion.21 = (bf16[4608,1536]{1,0:T(8,128)(2,1)}, bf16[4608,1536]{1,0:T(8,128)(2,1)}) fusion(bf16[4608,3072]{1,0:T(8,128)(2,1)} %reshape.35), kind=kLoop, calls=%fused_computation.24 | loop fusion | bytes 56623104 | tf_op jit(solution)/shard_map/slice | solution.py:28
  274.7 18.8 %copy.19 = bf16[4608,1536]{0,1:T(8,128)(2,1)} copy(bf16[4608,1536]{1,0:T(8,128)(2,1)} %get-tuple-element.2) | data formatting | bytes 28311552 | tf_op jit(solution)/shard_map/slice | solution.py:28
  293.5 6.2 %multiply_select_fusion = f32[12,4608,36]{1,2,0:T(8,128)S(1)} fusion(bf16[4608,12,128]{0,2,1:T(8,128)(2,1)} %bitcast.41, pred[4608]{0:T(1024)(128)(4,1)S(1)} %fusion.19, bf16[36,12,128]{2,1,0:T(8,128)(2,1)S(1)} %reshape_squeeze.3), kind=kOutput, calls=%fused_computation.5 | convolution fusion | flops 513589248 | bytes 22233600 | tf_op jit(solution)/shard_map/qhd,khd->hqk/dot_general | solution.py:32
  299.7 4.8 %fusion.22 = (f32[12,36]{1,0:T(8,128)S(1)}, bf16[12,36,4608]{2,1,0:T(8,128)(2,1)}) fusion(f32[12,4608,36]{1,2,0:T(8,128)S(1)} %multiply_select_fusion, pred[4608]{0:T(1024)(128)(4,1)S(1)} %fusion.19), kind=kOutput, calls=%fused_computation.25 | output fusion | flops 7967231 | bytes 11950272 | tf_op jit(solution)/shard_map/sub | solution.py:35
  304.5 18.5 %copy.22 = bf16[4608,1536]{0,1:T(8,128)(2,1)} copy(bf16[4608,1536]{1,0:T(8,128)(2,1)} %get-tuple-element.3) | data formatting | bytes 28311552 | tf_op jit(solution)/shard_map/slice | solution.py:29
  323.0 0.0 copy-start.2
  323.0 0.0 copy-start.3
  323.0 11.1 %fusion.15 = bf16[36,12,128]{2,0,1:T(8,128)(2,1)S(1)} fusion(bf16[4608,12,128]{0,2,1:T(8,128)(2,1)} %bitcast.42, bf16[12,36,4608]{2,1,0:T(8,128)(2,1)} %get-tuple-element.5, f32[36,12]{0,1:T(8,128)S(1)} %bitcast.50), kind=kOutput, calls=%fused_computation.13 | convolution fusion | flops 509718528 | bytes 18249408 | tf_op jit(solution)/shard_map/hqk,khd->hqd/dot_general | solution.py:37
  334.2 0.0 copy-start.5
  334.3 0.0 copy-done.2
  334.3 0.0 copy-done.3
  334.3 0.0 copy-start.4
  334.3 5.4 %fusion.8 = bf16[36,3072]{1,0:T(8,128)(2,1)S(1)} fusion(bf16[36,1536]{1,0:T(8,128)(2,1)S(1)} %bitcast.44, bf16[1536,3072]{1,0:T(8,128)(2,1)} %param.16, bf16[1,36,3072]{2,1,0:T(8,128)(2,1)S(1)} %copy-done.2, f32[3072]{0:T(1024)S(1)} %bitcast.49), kind=kOutput, calls=%fused_computation.10 | convolution fusion | flops 340180992 | bytes 10002432 | tf_op jit(solution)/shard_map/dot_general | solution.py:41
  339.7 0.0 copy-done
  339.7 0.0 copy-start.1
  339.7 0.2 fusion.23
  340.0 0.3 collective-permute-start
  340.3 2.4 collective-permute-done
  342.7 0.6 add_bitcast_fusion
  343.3 0.0 all-gather.7.cloned.1.call-update
  343.3 0.0 copy-done.5
  343.3 0.6 fusion.20
  344.6 113.7 %all-gather.7.cloned.1.call-done = f32[128,36,64]{2,1,0:T(8,128)} async-done(((f32[1,36,64]{2,1,0:T(8,128)}), f32[128,36,64]{2,1,0:T(8,128)}) %all-gather.7.cloned.1.call-update) | async-done | bytes 1179664 | tf_op jit(solution)/shard_map/all_gather | solution.py:49
  458.3 2.4 reshape.37
  460.7 0.1 reshape.32
  460.8 0.0 copy-done.4
  460.8 0.6 sub.17
  461.4 0.0 copy-done.1
  (6 shorter events, 0.1 us)
Async XLA Ops:
  7.2 332.6 %copy-start = (bf16[3072,64]{0,1:T(8,128)(2,1)S(1)}, bf16[3072,64]{0,1:T(8,128)(2,1)}, u32[]{:S(2)}) copy-start(bf16[3072,64]{0,1:T(8,128)(2,1)} %param.17) | copy-start | bytes 1179652
  7.2 213.5 %all-gather.5.cloned.1.call-start = ((), (), s32[]{:S(2)}) async-start(), calls=%async_computation | async-start | bytes 31703040 | tf_op jit(solution)/shard_map/all_gather | solution.py:26
  9.0 449.3 %all-gather.7.cloned.1.call-start = ((), (), s32[]{:S(2)}) async-start(), calls=%async_computation.1 | async-start | bytes 2641920 | tf_op jit(solution)/shard_map/all_gather | solution.py:49
  323.0 11.2 %copy-start.2 = (bf16[1,36,3072]{2,1,0:T(8,128)(2,1)S(1)}, bf16[1,36,3072]{2,1,0:T(8,128)(2,1)}, u32[]{:S(2)}) copy-start(bf16[1,36,3072]{2,1,0:T(8,128)(2,1)} %param.13) | copy-start | bytes 663556
  323.0 11.2 %copy-start.3 = (f32[1,3072]{1,0:T(1,128)S(1)}, f32[1,3072]{1,0:T(1,128)}, u32[]{:S(2)}) copy-start(f32[1,3072]{1,0:T(1,128)} %param.14) | copy-start | bytes 36868
  334.2 9.1 %copy-start.5 = (s32[128]{0:T(128)S(1)}, s32[128]{0:T(128)}, u32[]{:S(2)}) copy-start(s32[128]{0:T(128)} %param.19) | copy-start | bytes 1540
  334.3 126.5 %copy-start.4 = (f32[1,1024]{1,0:T(1,128)S(1)}, f32[1,1024]{1,0:T(1,128)}, u32[]{:S(2)}) copy-start(f32[1,1024]{1,0:T(1,128)} %param.18) | copy-start | bytes 12292
  339.7 121.7 %copy-start.1 = (bf16[36,3072]{1,0:T(8,128)(2,1)}, bf16[36,3072]{1,0:T(8,128)(2,1)S(1)}, u32[]{:S(2)}) copy-start(bf16[36,3072]{1,0:T(8,128)(2,1)S(1)} %fusion.8) | copy-start | bytes 663556
  340.0 2.7 collective-permute-start
Sparse Core Ops, SparseCore 0:
  12.4 208.1 all-gather.4
  343.4 114.8 all-gather.6
where the time goes:
time: 470 us; the launch traced here: 468 us
  waiting for transfers between devices  326 us (69%)
  local copies, waits for them, and re-layouts  95 us (20%)
  matrix products  22.9 us (5%)
  between operations  15.5 us (3%)
  other arithmetic  8.35 us (2%)
    all_gather x1, waiting for transfers between devices, local(): lax.all_gather(jnp.concatenate([kloc, vloc], axis=1), 'seq', axis=0, tile...  210 us
    all_gather x1, waiting for transfers between devices, local(): gathered = lax.all_gather(guided, 'seq', axis=0, tiled=True)  114 us
    slice x2, local copies, waits for them, and re-layouts, local(): kall = both[:, :width].reshape(seqlen, HEADS, HEAD)  39.4 us
    unnamed x16, local copies, waits for them, and re-layouts  35.9 us
    slice x1, local copies, waits for them, and re-layouts, local(): vall = both[:, width:].reshape(seqlen, HEADS, HEAD)  18.5 us
    dot_general x1, matrix products, local(): jnp.einsum('hqk,khd->hqd', expo.astype(jnp.bfloat16), vall, preferred_ele...  11.1 us
  transfers between devices with their start and end apart: 3, of which 3 were waited for; matrix products, arithmetic and copies ran while one was open for 0% of the time, Pallas kernels for 0%

commit v1 on v0

--- a/solution.py
+++ b/solution.py
@@ -23,7 +23,12 @@
     textslots = seqlen // 9
     limit = text_len[0]
     scale = HEAD ** (-0.5)
-    both = lax.all_gather(jnp.concatenate([kloc, vloc], axis=1), "seq", axis=0, tiled=True)
+    both = jnp.concatenate(
+        lax.all_to_all(
+            jnp.stack([jnp.concatenate([kloc, vloc], axis=1)] * lax.axis_size("seq")), "seq", 0, 0
+        ),
+        axis=0,
+    )
     qheads = qloc.reshape(tokens, HEADS, HEAD)
     kall = both[:, :width].reshape(seqlen, HEADS, HEAD)
     vall = both[:, width:].reshape(seqlen, HEADS, HEAD)

time: 470 us -> 989 us (2.10)
  waiting for transfers between devices: 326 us -> 819 us
  starting transfers between devices: 0.41 us -> 17 us
  local copies, waits for them, and re-layouts: 95 us -> 105 us
    all_to_all x0 -> x1, waiting for transfers between devices: none -> 683 us  [local(): lax.all_to_all(jnp.stack([jnp.concatenate([kloc, vloc], axis=1)] * lax.ax...]
    all_gather x1 -> x0, waiting for transfers between devices: 210 us -> none  [local(): lax.all_gather(jnp.concatenate([kloc, vloc], axis=1), 'seq', axis=0, tile...]
    reshape x0 -> x1, local copies, waits for them, and re-layouts: none -> 33.4 us  [local(): jnp.concatenate(lax.all_to_all(jnp.stack([jnp.concatenate([kloc, vloc], a...]
    unnamed x16 -> x17, local copies, waits for them, and re-layouts: 35.9 us -> 2.54 us
    all_gather x1, waiting for transfers between devices: 114 us -> 133 us  [local(): gathered = lax.all_gather(guided, 'seq', axis=0, tiled=True)]
    all_to_all x0 -> x1, starting transfers between devices: none -> 16.9 us  [local(): lax.all_to_all(jnp.stack([jnp.concatenate([kloc, vloc], axis=1)] * lax.ax...]
    another operation x0 -> x1, local copies, waits for them, and re-layouts: none -> 10.6 us  [local(): jnp.stack([jnp.concatenate([kloc, vloc], axis=1)] * lax.axis_size('seq'))]
where the time goes in v1:
time: 989 us; the launch traced here: 987 us
  waiting for transfers between devices  819 us (83%)
  local copies, waits for them, and re-layouts  105 us (11%)
  matrix products  22.9 us (2%)
  starting transfers between devices  17 us (2%)
  between operations  15.5 us (2%)
    all_to_all x1, waiting for transfers between devices, local(): lax.all_to_all(jnp.stack([jnp.concatenate([kloc, vloc], axis=1)] * lax.ax...  683 us
    all_gather x1, waiting for transfers between devices, local(): gathered = lax.all_gather(guided, 'seq', axis=0, tiled=True)  133 us
    slice x2, local copies, waits for them, and re-layouts, local(): kall = both[:, :width].reshape(seqlen, HEADS, HEAD)  39.4 us
    reshape x1, local copies, waits for them, and re-layouts, local(): jnp.concatenate(lax.all_to_all(jnp.stack([jnp.concatenate([kloc, vloc], a...  33.4 us
  transfers between devices with their start and end apart: 3, of which 3 were waited for; matrix products, arithmetic and copies ran while one was open for 0% of the time, Pallas kernels for 0%

profile of v1, /device:TPU:1, one launch (start us, length us, event | category | flops | bytes accessed | tf_op | source)
XLA Modules:
  0.0 986.7 jit_solution(7105391379180451074)
XLA Ops:
  7.2 0.0 copy-start
  7.2 1.0 pad_maximum_fusion
  8.2 10.6 %stack.2 = bf16[128,36,3072]{2,1,0:T(8,128)(2,1)} broadcast(bf16[36,3072]{1,0:T(8,128)(2,1)S(1)} %pad_maximum_fusion), dimensions={1,2} | broadcast | bytes 28532736 | tf_op jit(solution)/shard_map/stack | solution.py:28
  18.8 0.0 copy-start.3
  18.8 16.9 %all-to-all-start = ((bf16[128,36,3072]{2,1,0:T(8,128)(2,1)}), bf16[128,36,3072]{2,1,0:T(8,128)(2,1)}, u32[]{:S(2)}, u32[]{:S(2)}) async-start(bf16[128,36,3072]{2,1,0:T(8,128)(2,1)} %stack.2), calls=%async_computation | async-start | bytes 62914560 | tf_op jit(solution)/shard_map/all_to_all | solution.py:27
  35.7 0.0 all-gather.3.cloned.1.call-start
  36.4 0.0 copy-done.3
  36.4 0.1 reshape_squeeze.3
  36.5 682.8 %all-to-all-done = bf16[128,36,3072]{2,1,0:T(8,128)(2,1)} async-done(((bf16[128,36,3072]{2,1,0:T(8,128)(2,1)}), bf16[128,36,3072]{2,1,0:T(8,128)(2,1)}, u32[]{:S(2)}, u32[]{:S(2)}) %all-to-all-start) | async-done | bytes 28311584 | tf_op jit(solution)/shard_map/all_to_all | solution.py:27
  719.3 33.4 %reshape.34 = bf16[4608,3072]{1,0:T(8,128)(2,1)} reshape(bf16[128,36,3072]{2,1,0:T(8,128)(2,1)} %all-to-all-done) | data formatting | bytes 56623104 | tf_op jit(solution)/shard_map/reshape | solution.py:26
  752.7 20.7 %fusion.21 = (bf16[4608,1536]{1,0:T(8,128)(2,1)}, bf16[4608,1536]{1,0:T(8,128)(2,1)}) fusion(bf16[4608,3072]{1,0:T(8,128)(2,1)} %reshape.34), kind=kLoop, calls=%fused_computation.24 | loop fusion | bytes 56623104 | tf_op jit(solution)/shard_map/slice | solution.py:33
  773.4 18.8 %copy.19 = bf16[4608,1536]{0,1:T(8,128)(2,1)} copy(bf16[4608,1536]{1,0:T(8,128)(2,1)} %get-tuple-element.2) | data formatting | bytes 28311552 | tf_op jit(solution)/shard_map/slice | solution.py:33
  792.1 6.2 multiply_select_fusion
  798.3 4.8 fusion.22
  803.1 18.5 %copy.22 = bf16[4608,1536]{0,1:T(8,128)(2,1)} copy(bf16[4608,1536]{1,0:T(8,128)(2,1)} %get-tuple-element.3) | data formatting | bytes 28311552 | tf_op jit(solution)/shard_map/slice | solution.py:34
  821.7 0.0 copy-start.2
  821.7 0.0 copy-start.4
  821.7 11.1 %fusion.15 = bf16[36,12,128]{2,0,1:T(8,128)(2,1)S(1)} fusion(bf16[4608,12,128]{0,2,1:T(8,128)(2,1)} %bitcast.40, bf16[12,36,4608]{2,1,0:T(8,128)(2,1)} %get-tuple-element.5, f32[36,12]{0,1:T(8,128)S(1)} %bitcast.48), kind=kOutput, calls=%fused_computation.13 | convolution fusion | flops 509718528 | bytes 18249408 | tf_op jit(solution)/shard_map/hqk,khd->hqd/dot_general | solution.py:42
  832.8 0.0 copy-start.6
  832.9 0.0 copy-done.2
  832.9 0.0 copy-done.4
  832.9 0.0 copy-start.5
  832.9 5.4 fusion.8
  838.4 0.0 copy-done
  838.4 0.0 copy-start.1
  838.4 0.2 fusion.23
  838.6 0.1 collective-permute-start
  838.7 2.6 collective-permute-done
  841.3 0.6 add_bitcast_fusion
  841.9 0.0 all-gather.3.cloned.1.call-update
  841.9 0.0 copy-done.6
  841.9 0.6 fusion.20
  843.2 133.5 %all-gather.3.cloned.1.call-done = f32[128,36,64]{2,1,0:T(8,128)} async-done(((f32[1,36,64]{2,1,0:T(8,128)}), f32[128,36,64]{2,1,0:T(8,128)}) %all-gather.3.cloned.1.call-update) | async-done | bytes 1179664 | tf_op jit(solution)/shard_map/all_gather | solution.py:54
  976.7 2.4 reshape.41
  979.2 0.1 reshape.38
  979.2 0.0 copy-done.5
  979.3 0.6 sub.17
  979.9 0.0 copy-done.1
  (6 shorter events, 0.1 us)
Async XLA Ops:
  7.2 831.2 %copy-start = (bf16[3072,64]{0,1:T(8,128)(2,1)S(1)}, bf16[3072,64]{0,1:T(8,128)(2,1)}, u32[]{:S(2)}) copy-start(bf16[3072,64]{0,1:T(8,128)(2,1)} %param.17) | copy-start | bytes 1179652
  18.8 17.6 %copy-start.3 = (bf16[1,36,1536]{2,1,0:T(8,128)(2,1)S(1)}, bf16[1,36,1536]{2,1,0:T(8,128)(2,1)}, u32[]{:S(2)}) copy-start(bf16[1,36,1536]{2,1,0:T(8,128)(2,1)} %param.10) | copy-start | bytes 331780
  18.8 700.5 %all-to-all-start = ((bf16[128,36,3072]{2,1,0:T(8,128)(2,1)}), bf16[128,36,3072]{2,1,0:T(8,128)(2,1)}, u32[]{:S(2)}, u32[]{:S(2)}) async-start(bf16[128,36,3072]{2,1,0:T(8,128)(2,1)} %stack.2), calls=%async_computation | async-start | bytes 62914560 | tf_op jit(solution)/shard_map/all_to_all | solution.py:27
  35.7 941.0 %all-gather.3.cloned.1.call-start = ((), (), s32[]{:S(2)}) async-start(), calls=%async_computation.1 | async-start | bytes 2641920 | tf_op jit(solution)/shard_map/all_gather | solution.py:54
  821.7 11.2 %copy-start.2 = (bf16[1,36,3072]{2,1,0:T(8,128)(2,1)S(1)}, bf16[1,36,3072]{2,1,0:T(8,128)(2,1)}, u32[]{:S(2)}) copy-start(bf16[1,36,3072]{2,1,0:T(8,128)(2,1)} %param.13) | copy-start | bytes 663556
  821.7 11.2 %copy-start.4 = (f32[1,3072]{1,0:T(1,128)S(1)}, f32[1,3072]{1,0:T(1,128)}, u32[]{:S(2)}) copy-start(f32[1,3072]{1,0:T(1,128)} %param.14) | copy-start | bytes 36868
  832.8 9.1 copy-start.6
  832.9 146.3 %copy-start.5 = (f32[1,1024]{1,0:T(1,128)S(1)}, f32[1,1024]{1,0:T(1,128)}, u32[]{:S(2)}) copy-start(f32[1,1024]{1,0:T(1,128)} %param.18) | copy-start | bytes 12292
  838.4 141.5 %copy-start.1 = (bf16[36,3072]{1,0:T(8,128)(2,1)}, bf16[36,3072]{1,0:T(8,128)(2,1)S(1)}, u32[]{:S(2)}) copy-start(bf16[36,3072]{1,0:T(8,128)(2,1)S(1)} %fusion.8) | copy-start | bytes 663556
  838.6 2.7 collective-permute-start
Sparse Core Ops, SparseCore 0:
  842.1 134.6 all-gather.2
